TPU v7x, 32 devices: a whole 2x2x4 slice. The times are simulated.
32 devices in a mesh: dp: 16 (over z, y, core), tensor: 2 (over x).
Axes of the slice: x: 2, y: 2, z: 4, core: 2. Of those that a mesh axis runs over, the one named last changes fastest.
Arguments:
- hidden_in: bfloat16 [4096, 1024], P(('dp', 'tensor')), may hold values from -6 to 6
- out_grad: bfloat16 [4096, 1024], P(('dp', 'tensor')), may hold values from -6 to 6
- span_start: int32 [16, 2], P('dp'), may hold values from 0 to 240, as said below
- span_length: int32 [16, 2], P('dp'), may hold values from 16 to 128
- attn_gain: bfloat16 [1024], P(('dp', 'tensor')), may hold values from 0.099609375 to 1.8984375
- attn_shift: bfloat16 [1024], P(('dp', 'tensor')), may hold values from -3 to 3
- mlp_gain: bfloat16 [1024], P(('dp', 'tensor')), may hold values from 0.099609375 to 1.8984375
- mlp_shift: bfloat16 [1024], P(('dp', 'tensor')), may hold values from -3 to 3
- qkv_weight: bfloat16 [1024, 3, 1024], P('dp', None, 'tensor'), may hold values from -0.1875 to 0.1875
- qkv_bias: bfloat16 [3, 1024], P(None, ('tensor', 'dp')), may hold values from -3 to 3
- dense_weight: bfloat16 [1024, 1024], P(('tensor', 'dp')), may hold values from -1.5 to 1.5
- dense_bias: bfloat16 [1024], P(('dp', 'tensor')), may hold values from -3 to 3
- up_weight: bfloat16 [1024, 4096], P('dp', 'tensor'), may hold values from -0.1875 to 0.1875
- up_bias: bfloat16 [4096], P(('tensor', 'dp')), may hold values from -3 to 3
- down_weight: bfloat16 [4096, 1024], P(('tensor', 'dp')), may hold values from -0.09375 to 0.09375
- down_bias: bfloat16 [1024], P(('dp', 'tensor')), may hold values from -3 to 3
Outputs:
- layer_out: bfloat16 [4096, 1024], P(('dp', 'tensor'))
- input_grad: bfloat16 [4096, 1024], P(('dp', 'tensor'))
- attn_gain_grad: float32 [1024], P(('dp', 'tensor'))
- attn_shift_grad: float32 [1024], P(('dp', 'tensor'))
- mlp_gain_grad: float32 [1024], P(('dp', 'tensor'))
- mlp_shift_grad: float32 [1024], P(('dp', 'tensor'))
- qkv_weight_grad: float32 [1024, 3, 1024], P('dp', None, 'tensor')
- qkv_bias_grad: float32 [3, 1024], P(None, ('tensor', 'dp'))
- dense_weight_grad: float32 [1024, 1024], P(('tensor', 'dp'))
- dense_bias_grad: float32 [1024], P(('dp', 'tensor'))
- up_weight_grad: float32 [1024, 4096], P('dp', 'tensor')
- up_bias_grad: float32 [4096], P(('tensor', 'dp'))
- down_weight_grad: float32 [4096, 1024], P(('tensor', 'dp'))
- down_bias_grad: float32 [1024], P(('dp', 'tensor'))
Inputs may be any that keep to these rules, and one draw needn't show every extreme that they name: `span_start`: span slot k of a sequence lies inside its positions k * 128 to (k + 1) * 128 - 1.
All inputs are finite; a program needn't handle non-finite values.
Results may differ from a plain program's by a relative error of at most 0.011.
Values may be sent and summed in bfloat16 or wider, within the bound.
A program may use at most 128 MiB of HBM per device.

v0:
```python
import jax
import jax.numpy as jnp
from jax import lax
from jax.sharding import PartitionSpec as P

HD = 64
ROT = 16
NORM_EPS = 1e-05
NEG_FILL = -1000000000.0


def layer_norm(rows_in, gain_vec, shift_vec):
    mean_row = jnp.mean(rows_in, axis=-1, keepdims=True)
    centred = rows_in - mean_row
    spread = jnp.mean(centred * centred, axis=-1, keepdims=True)
    return centred * lax.rsqrt(spread + NORM_EPS) * gain_vec + shift_vec


def rotary_tables(length):
    position = jnp.arange(length, dtype=jnp.float32)
    rates = 10000.0 ** (-jnp.arange(ROT // 2, dtype=jnp.float32) * (2.0 / ROT))
    angles = position[:, None] * rates[None, :]
    angles = jnp.concatenate([angles, angles], axis=-1)[:, None, :]
    return (jnp.cos(angles), jnp.sin(angles))


def rotate(field_in, cosine, sines):
    turned = field_in[..., :ROT]
    first_half = turned[..., : ROT // 2]
    second_half = turned[..., ROT // 2 :]
    swapped = jnp.concatenate([-second_half, first_half], axis=-1)
    return jnp.concatenate([turned * cosine + swapped * sines, field_in[..., ROT:]], axis=-1)


def gelu_exact(values_in):
    return jax.nn.gelu(values_in, approximate=False)


def shards(
    hidden_in,
    out_grad,
    span_start,
    span_length,
    attn_gain,
    attn_shift,
    mlp_gain,
    mlp_shift,
    qkv_weight,
    qkv_bias,
    dense_weight,
    dense_bias,
    up_weight,
    up_bias,
    down_weight,
    down_bias,
):
    local_rows = hidden_in.shape[0]
    length = local_rows * lax.axis_size("tensor")
    block_rows = min(512, length)
    block_count = length // block_rows
    score_scale = HD ** (-0.5)
    small_full = (
        lax.all_gather(attn_gain, ("dp", "tensor"), axis=0, tiled=True),
        lax.all_gather(attn_shift, ("dp", "tensor"), axis=0, tiled=True),
        lax.all_gather(mlp_gain, ("dp", "tensor"), axis=0, tiled=True),
        lax.all_gather(mlp_shift, ("dp", "tensor"), axis=0, tiled=True),
        lax.all_gather(dense_bias, ("dp", "tensor"), axis=0, tiled=True),
        lax.all_gather(down_bias, ("dp", "tensor"), axis=0, tiled=True),
    )
    small_vecs = [item.astype(jnp.float32) for item in small_full]
    own_rows = hidden_in.astype(jnp.float32)
    normed_attn = layer_norm(own_rows, small_vecs[0], small_vecs[1]).astype(jnp.bfloat16)
    normed_mlp = layer_norm(own_rows, small_vecs[2], small_vecs[3]).astype(jnp.bfloat16)
    attn_full, mlp_full = (
        lax.all_gather(normed_attn, "tensor", axis=0, tiled=True),
        lax.all_gather(normed_mlp, "tensor", axis=0, tiled=True),
    )
    full_qkv, full_qkv_bias, full_dense, full_up, full_up_bias, full_down = (
        lax.all_gather(qkv_weight, "dp", axis=0, tiled=True),
        lax.all_gather(qkv_bias, "dp", axis=1, tiled=True),
        lax.all_gather(dense_weight, "dp", axis=0, tiled=True),
        lax.all_gather(up_weight, "dp", axis=0, tiled=True),
        lax.all_gather(up_bias, "dp", axis=0, tiled=True),
        lax.all_gather(down_weight, "dp", axis=0, tiled=True),
    )
    model_width = full_qkv.shape[0]
    head_cols = full_qkv.shape[2]
    local_heads = head_cols // HD
    projected = jnp.dot(
        attn_full, full_qkv.reshape(model_width, 3 * head_cols), preferred_element_type=jnp.float32
    )
    projected = projected + full_qkv_bias.reshape(3 * head_cols).astype(jnp.float32)
    projected = projected.reshape(length, 3, local_heads, HD)
    cosine, sines = rotary_tables(length)
    query_rows = rotate(projected[:, 0], cosine, sines).astype(jnp.bfloat16)
    key_rows = rotate(projected[:, 1], cosine, sines).astype(jnp.bfloat16)
    value_rows = projected[:, 2].astype(jnp.bfloat16)
    position = jnp.arange(length, dtype=jnp.int32)
    starts_here = span_start[0]
    lengths_here = span_length[0]
    inside = (position[None, :] >= starts_here[:, None]) & (
        position[None, :] < (starts_here + lengths_here)[:, None]
    )
    marks = (jnp.arange(starts_here.shape[0], dtype=jnp.int32) + 1)[:, None]
    labels = jnp.sum(jnp.where(inside, marks, 0), axis=0)

    def block_scores(first_row, query_block):
        raw_scores = (
            jnp.einsum("qhe,khe->hqk", query_block, key_rows, preferred_element_type=jnp.float32)
            * score_scale
        )
        row_pos = first_row + jnp.arange(block_rows, dtype=jnp.int32)
        allowed = (position[None, :] <= row_pos[:, None]) | (labels[:, None] == labels[None, :]) & (
            labels[:, None] > 0
        )
        return jnp.where(allowed[None], raw_scores, NEG_FILL)

    def attend(first_row):
        scores = block_scores(first_row, query_rows)
        row_top = jnp.max(scores, axis=-1, keepdims=True)
        exponent = jnp.exp(scores - row_top)
        summed = jnp.sum(exponent, axis=-1, keepdims=True)
        prob_low = (exponent / summed).astype(jnp.bfloat16)
        context_block = jnp.einsum(
            "hqk,khe->qhe", prob_low, value_rows, preferred_element_type=jnp.float32
        )
        return (context_block.astype(jnp.bfloat16), (row_top + jnp.log(summed))[..., 0])

    block_starts = jnp.arange(block_count, dtype=jnp.int32) * block_rows
    context_blocks, lse_blocks = lax.map(attend, block_starts)
    context = context_blocks.reshape(length, head_cols)
    attn_part = jnp.dot(context, full_dense, preferred_element_type=jnp.float32)
    attn_mixed = lax.psum_scatter(
        attn_part.astype(jnp.bfloat16), "tensor", scatter_dimension=0, tiled=True
    ).astype(jnp.float32)
    hidden = jnp.dot(mlp_full, full_up, preferred_element_type=jnp.float32) + full_up_bias.astype(
        jnp.float32
    )
    active = gelu_exact(hidden).astype(jnp.bfloat16)
    mlp_part = jnp.dot(active, full_down, preferred_element_type=jnp.float32)
    mixed_rows = attn_mixed + lax.psum_scatter(
        mlp_part.astype(jnp.bfloat16), "tensor", scatter_dimension=0, tiled=True
    ).astype(jnp.float32)
    layer_out = (own_rows + mixed_rows + small_vecs[4] + small_vecs[5]).astype(jnp.bfloat16)
    cot_full = lax.all_gather(out_grad, "tensor", axis=0, tiled=True)
    full_qkv, full_dense, full_up, full_down = (
        lax.all_gather(qkv_weight, "dp", axis=0, tiled=True),
        lax.all_gather(dense_weight, "dp", axis=0, tiled=True),
        lax.all_gather(up_weight, "dp", axis=0, tiled=True),
        lax.all_gather(down_weight, "dp", axis=0, tiled=True),
    )
    down_grad = jnp.einsum("lf,ld->fd", active, cot_full, preferred_element_type=jnp.float32)
    dense_grad = jnp.einsum("le,ld->ed", context, cot_full, preferred_element_type=jnp.float32)
    active_grad = jnp.einsum("ld,fd->lf", cot_full, full_down, preferred_element_type=jnp.float32)
    hidden_grad = jax.vjp(gelu_exact, hidden)[1](active_grad)[0].astype(jnp.bfloat16)
    up_grad = jnp.einsum("ld,lf->df", mlp_full, hidden_grad, preferred_element_type=jnp.float32)
    up_bias_grad = jnp.sum(hidden_grad, axis=0, dtype=jnp.float32)
    mlp_in_grad = jnp.einsum("lf,df->ld", hidden_grad, full_up, preferred_element_type=jnp.float32)
    context_grad = jnp.einsum("ld,ed->le", cot_full, full_dense, preferred_element_type=jnp.float32)
    context_grad = context_grad.astype(jnp.bfloat16).reshape(length, local_heads, HD)

    def attend_back(carried, inputs):
        key_acc, value_acc = carried
        first_row, lse_block = inputs
        scores = block_scores(first_row, query_rows)
        prob_rows = jnp.exp(scores - lse_block[..., None])
        prob_low = prob_rows.astype(jnp.bfloat16)
        value_acc = value_acc + jnp.einsum(
            "hqk,qhe->khe", prob_low, context_grad, preferred_element_type=jnp.float32
        )
        prob_grad = jnp.einsum(
            "qhe,khe->hqk", context_grad, value_rows, preferred_element_type=jnp.float32
        )
        score_grad = prob_rows * (
            prob_grad - jnp.sum(prob_grad * prob_rows, axis=-1, keepdims=True)
        )
        score_grad = score_grad.astype(jnp.bfloat16)
        query_grad = (
            jnp.einsum("hqk,khe->qhe", score_grad, key_rows, preferred_element_type=jnp.float32)
            * score_scale
        )
        key_acc = (
            key_acc
            + jnp.einsum("hqk,qhe->khe", score_grad, query_rows, preferred_element_type=jnp.float32)
            * score_scale
        )
        return ((key_acc, value_acc), query_grad)

    zero_rows = jnp.zeros((length, local_heads, HD), jnp.float32)
    (key_grad, value_grad), query_blocks = lax.scan(
        attend_back, (zero_rows, zero_rows), (block_starts, lse_blocks)
    )
    query_grad = query_blocks.reshape(length, local_heads, HD)

    def turn(field_in):
        return rotate(field_in, cosine, sines)

    turn_back = jax.vjp(turn, zero_rows)[1]
    projected_grad = jnp.stack(
        [turn_back(query_grad)[0], turn_back(key_grad)[0], value_grad], axis=1
    )
    projected_grad = projected_grad.astype(jnp.bfloat16).reshape(length, 3 * head_cols)
    qkv_weight_grad = jnp.einsum(
        "ld,lc->dc", attn_full, projected_grad, preferred_element_type=jnp.float32
    )
    qkv_weight_grad = qkv_weight_grad.reshape(model_width, 3, head_cols)
    qkv_bias_grad = jnp.sum(projected_grad, axis=0, dtype=jnp.float32).reshape(3, head_cols)
    attn_in_grad = jnp.einsum(
        "lc,dc->ld",
        projected_grad,
        full_qkv.reshape(model_width, 3 * head_cols),
        preferred_element_type=jnp.float32,
    )
    reduced = (
        lax.psum_scatter(qkv_weight_grad, "dp", scatter_dimension=0, tiled=True),
        lax.psum_scatter(qkv_bias_grad, "dp", scatter_dimension=1, tiled=True),
        lax.psum_scatter(dense_grad, "dp", scatter_dimension=0, tiled=True),
        lax.psum_scatter(up_grad, "dp", scatter_dimension=0, tiled=True),
        lax.psum_scatter(up_bias_grad, "dp", scatter_dimension=0, tiled=True),
        lax.psum_scatter(down_grad, "dp", scatter_dimension=0, tiled=True),
    )
    attn_local, mlp_local = (
        lax.psum_scatter(
            attn_in_grad.astype(jnp.bfloat16), "tensor", scatter_dimension=0, tiled=True
        ).astype(jnp.float32),
        lax.psum_scatter(
            mlp_in_grad.astype(jnp.bfloat16), "tensor", scatter_dimension=0, tiled=True
        ).astype(jnp.float32),
    )
    pull_attn = jax.vjp(layer_norm, own_rows, small_vecs[0], small_vecs[1])[1]
    pull_mlp = jax.vjp(layer_norm, own_rows, small_vecs[2], small_vecs[3])[1]
    rows_grad_attn, gain_grad_attn, shift_grad_attn = pull_attn(attn_local)
    rows_grad_mlp, gain_grad_mlp, shift_grad_mlp = pull_mlp(mlp_local)
    cot_rows = out_grad.astype(jnp.float32)
    input_grad = (cot_rows + rows_grad_attn + rows_grad_mlp).astype(jnp.bfloat16)
    bias_total = jnp.sum(cot_rows, axis=0)
    small_sums = (
        lax.psum_scatter(gain_grad_attn, ("dp", "tensor"), scatter_dimension=0, tiled=True),
        lax.psum_scatter(shift_grad_attn, ("dp", "tensor"), scatter_dimension=0, tiled=True),
        lax.psum_scatter(gain_grad_mlp, ("dp", "tensor"), scatter_dimension=0, tiled=True),
        lax.psum_scatter(shift_grad_mlp, ("dp", "tensor"), scatter_dimension=0, tiled=True),
        lax.psum_scatter(bias_total, ("dp", "tensor"), scatter_dimension=0, tiled=True),
    )
    return (
        layer_out,
        input_grad,
        small_sums[0],
        small_sums[1],
        small_sums[2],
        small_sums[3],
        reduced[0],
        reduced[1],
        reduced[2],
        small_sums[4],
        reduced[3],
        reduced[4],
        reduced[5],
        small_sums[4],
    )


def solution(mesh):
    in_specs = (
        P(("dp", "tensor"), None),
        P(("dp", "tensor"), None),
        P("dp", None),
        P("dp", None),
        P(("dp", "tensor")),
        P(("dp", "tensor")),
        P(("dp", "tensor")),
        P(("dp", "tensor")),
        P("dp", None, "tensor"),
        P(None, ("tensor", "dp")),
        P(("tensor", "dp"), None),
        P(("dp", "tensor")),
        P("dp", "tensor"),
        P(("tensor", "dp")),
        P(("tensor", "dp"), None),
        P(("dp", "tensor")),
    )
    out_specs = (
        P(("dp", "tensor"), None),
        P(("dp", "tensor"), None),
        P(("dp", "tensor")),
        P(("dp", "tensor")),
        P(("dp", "tensor")),
        P(("dp", "tensor")),
        P("dp", None, "tensor"),
        P(None, ("tensor", "dp")),
        P(("tensor", "dp"), None),
        P(("dp", "tensor")),
        P("dp", "tensor"),
        P(("tensor", "dp")),
        P(("tensor", "dp"), None),
        P(("dp", "tensor")),
    )
    return jax.shard_map(shards, mesh=mesh, in_specs=in_specs, out_specs=out_specs, check_vma=False)
```

profile of v0, /device:TPU:0, one launch (start us, length us, event | category | flops | bytes accessed | tf_op | source)
XLA Modules:
  0.0 704.2 jit_solution(13958768486302023803)
XLA Ops:
  7.2 0.7 all-gather.9.cloned.1.call-update
  8.0 0.7 all-gather.7.cloned.1.call-update
  8.7 0.7 all-gather.11.cloned.1.call-update
  10.0 0.8 dynamic-update-slice
  10.9 0.8 dynamic-update-slice.1
  11.7 0.8 dynamic-update-slice.2
  12.6 0.8 dynamic-update-slice.3
  13.4 0.8 dynamic-update-slice.4
  14.2 0.8 dynamic-update-slice.5
  15.1 42.2 %all-reduce.21 = (bf16[1024]{0:T(1024)(128)(2,1)S(1)}, bf16[1024]{0:T(1024)(128)(2,1)S(1)}, bf16[1024]{0:T(1024)(128)(2,1)S(1)}, bf16[1024]{0:T(1024)(128)(2,1)S...) all-reduce(bf16[1024]{0:T(1024)(128)(2,1)S(1)} %dynamic-update-slic, ...), channel_id=1, replica_groups=mesh['dp'=16,'tensor'=2] {'dp','tensor'}, use_global_device_ids=true, to_apply=%add.11 | all-reduce | flops 6144 | bytes 24576
  57.3 21.3 %all-gather = bf16[16,32,3]{1,2,0:T(4,128)(2,1)S(1)} all-gather(bf16[1,32,3]{1,2,0:T(4,128)(2,1)} %bitcast.96), channel_id=1, replica_groups=mesh['dp'=16,'tensor'=2] {'dp'}, dimensions={0}, use_global_device_ids=true | all-gather | bytes 3264 | tf_op jit(solution)/shard_map/all_gather | solution.py:80
  78.7 17.6 %all-gather.1 = bf16[16,1,128]{2,1,0:T(2,128)(2,1)S(1)} all-gather(bf16[1,1,128]{2,1,0:T(2,128)(2,1)} %bitcast.97), channel_id=1, replica_groups=mesh['dp'=16,'tensor'=2] {'dp'}, dimensions={0}, use_global_device_ids=true | all-gather | bytes 4352 | tf_op jit(solution)/shard_map/all_gather | solution.py:83
  96.5 0.7 bitcast_add_fusion
  97.1 0.7 fusion.51
  97.9 1.1 convert_reduce_fusion.4
  99.0 1.2 fusion.28
  100.1 1.2 fusion.25
  101.4 9.2 %all_gather.51 = bf16[256,1024]{1,0:T(8,128)(2,1)S(1)} all-gather(bf16[128,1024]{1,0:T(8,128)(2,1)S(1)} %get-tuple-element.105), channel_id=1, replica_groups=mesh['dp'=16,'tensor'=2] {'tensor'}, dimensions={0}, use_global_device_ids=true | all-gather | bytes 786432 | tf_op jit(solution)/shard_map/all_gather | solution.py:75
  110.6 8.5 %all_gather.63 = bf16[256,1024]{1,0:T(8,128)(2,1)S(1)} all-gather(bf16[128,1024]{1,0:T(8,128)(2,1)S(1)} %copy-done.9), channel_id=1, replica_groups=mesh['dp'=16,'tensor'=2] {'tensor'}, dimensions={0}, use_global_device_ids=true | all-gather | bytes 786432 | tf_op jit(solution)/shard_map/all_gather | solution.py:145
  119.0 7.7 %all_gather.57 = bf16[256,1024]{1,0:T(8,128)(2,1)} all-gather(bf16[128,1024]{1,0:T(8,128)(2,1)S(1)} %get-tuple-element.106), channel_id=1, replica_groups=mesh['dp'=16,'tensor'=2] {'tensor'}, dimensions={0}, use_global_device_ids=true | all-gather | bytes 786432 | tf_op jit(solution)/shard_map/all_gather | solution.py:76
  126.9 1.7 convolution_convert_fusion.4
  128.6 0.8 copy.71
  129.4 4.7 copy.67
  134.1 4.1 convolution_add_fusion
  138.2 1.9 copy.69
  140.4 0.9 copy-done.1
  142.3 1.6 multiply_reduce_fusion
  146.1 0.9 copy.84
  147.0 3.8 convolution_convert_fusion.2
  151.1 5.0 convolution_add_fusion.1
  156.1 44.1 %all-gather.13.cloned.1.call-done = bf16[2048,1024]{1,0:T(8,128)(2,1)} async-done(((bf16[128,1024]{1,0:T(8,128)(2,1)}), bf16[2048,1024]{1,0:T(8,128)(2,1)}) %all-gather.13.cloned.1.call-update) | async-done | bytes 4194320 | tf_op jit(solution)/shard_map/all_gather | solution.py:84
  200.2 9.0 %convert_reduce_fusion = (f32[2048]{0:T(1024)S(1)}, bf16[256,2048]{1,0:T(8,128)(2,1)S(1)}, f32[256,2048]{1,0:T(8,128)}) fusion(f32[256,2048]{1,0:T(8,128)} %convolution_add_fusion.1, bf16[256,1024]{1,0:T(8,128)(2,1)S(1)} %all_gather.63, bf16[2048,1024]{1,0:T(8,128)(2,1)} %all-gather.13.cloned.1.call-done), kind=kOutput, calls=%fused_computation.4 | convolution fusion | flops 1112537088 | bytes 9969664 | tf_op jit(solution)/shard_map/ld,fd->lf/dot_general | solution.py:154
  209.2 1.0 copy-done.7
  210.2 2.1 convolution_convert_fusion.1
  212.4 1.6 convolution_convert_fusion.5
  214.0 0.7 copy-done.11
  214.7 1.3 convolution_convert_fusion
  216.0 2.8 multiply_convert_fusion.1
  218.8 0.7 copy-done.13
  219.6 2.1 convolution_convert_fusion.3
  221.8 1.8 fusion.58
  223.6 3.7 fusion.36
  227.4 4.5 fusion.60
  232.0 1.0 copy-done.4
  233.3 4.5 fusion.59
  237.9 0.6 copy-done.15
  238.5 0.6 dynamic-slice.5
  239.7 18.3 %reduce-scatter.28.cloned.1.call-done = f32[32,3]{1,0:T(8,128)} async-done(((f32[512,3]{1,0:T(8,128)}), f32[32,3]{1,0:T(8,128)}) %reduce-scatter.28.cloned.1.call-update) | async-done | bytes 400
  258.0 1.4 copy.83
  259.3 30.2 %all-reduce.19 = f32[2048]{0:T(1024)S(1)} all-reduce(f32[2048]{0:T(1024)S(1)} %get-tuple-element.92), channel_id=15, replica_groups=mesh['dp'=16,'tensor'=2] {'dp'}, use_global_device_ids=true, to_apply=%region_30.31.clone | all-reduce | flops 2048 | bytes 16384
  289.5 0.6 dynamic-slice.6
  290.6 1.3 fusion.29
  292.0 1.6 fusion.35
  293.6 13.8 %reduce-scatter.12.cloned.1.call-done = bf16[128,1024]{1,0:T(8,128)(2,1)} async-done(((bf16[256,1024]{1,0:T(8,128)(2,1)}), bf16[128,1024]{1,0:T(8,128)(2,1)}) %reduce-scatter.12.cloned.1.call-update) | async-done | bytes 262160 | tf_op jit(solution)/shard_map/reduce_scatter | solution.py:133
  307.4 16.9 %reduce-scatter.14.cloned.1.call-done = bf16[128,1024]{1,0:T(8,128)(2,1)} async-done(((bf16[256,1024]{1,0:T(8,128)(2,1)}), bf16[128,1024]{1,0:T(8,128)(2,1)}) %reduce-scatter.14.cloned.1.call-update) | async-done | bytes 262160 | tf_op jit(solution)/shard_map/reduce_scatter | solution.py:141
  324.3 2.4 convert_reduce_fusion.5
  326.8 39.8 %all-reduce.20 = (f32[1024]{0:T(1024)S(1)}, f32[1024]{0:T(1024)S(1)}, f32[1024]{0:T(1024)S(1)}, f32[1024]{0:T(1024)S(1)}, f32[1024]{0:T(1024)S(1)}) all-reduce(f32[1024]{0:T(1024)S(1)} %get-tuple-element.76, f32[1024]{0:T(1024)S(1)} %get-tuple-element.80, ...), channel_id=6, replica_groups=mesh['dp'=16,'tensor'=2] {'dp','tensor'}, use_global_device_ids=true, to_apply=%region_15.16.clone | all-reduce | flops 5120 | bytes 40960
  366.6 0.6 dynamic-slice
  367.2 0.6 dynamic-slice.1
  367.8 0.6 dynamic-slice.2
  368.9 21.7 %reduce-scatter.22.cloned.1.call-done = f32[32,1024]{1,0:T(8,128)} async-done(((f32[512,1024]{1,0:T(8,128)}), f32[32,1024]{1,0:T(8,128)}) %reduce-scatter.22.cloned.1.call-update) | async-done | bytes 131088 | tf_op jit(solution)/shard_map/reduce_scatter | solution.py:217
  390.7 89.3 %reduce-scatter.20.cloned.1.call-done = f32[64,3,512]{2,0,1:T(8,128)} async-done(((f32[1024,3,512]{2,0,1:T(8,128)}), f32[64,3,512]{2,0,1:T(8,128)}) %reduce-scatter.20.cloned.1.call-update) | async-done | bytes 393232 | tf_op jit(solution)/shard_map/reduce_scatter | solution.py:215
  479.9 108.2 %reduce-scatter.26.cloned.1.call-done = f32[128,1024]{1,0:T(8,128)} async-done(((f32[2048,1024]{1,0:T(8,128)}), f32[128,1024]{1,0:T(8,128)}) %reduce-scatter.26.cloned.1.call-update) | async-done | bytes 524304 | tf_op jit(solution)/shard_map/reduce_scatter | solution.py:220
  588.1 109.0 %reduce-scatter.24.cloned.1.call-done = f32[64,2048]{1,0:T(8,128)} async-done(((f32[1024,2048]{1,0:T(8,128)}), f32[64,2048]{1,0:T(8,128)}) %reduce-scatter.24.cloned.1.call-update) | async-done | bytes 524304 | tf_op jit(solution)/shard_map/reduce_scatter | solution.py:218
  (107 shorter events, 7.2 us)
Async XLA Ops:
  7.2 103.4 %copy-start.9 = (bf16[128,1024]{1,0:T(8,128)(2,1)S(1)}, bf16[128,1024]{1,0:T(8,128)(2,1)}, u32[]{:S(2)}) copy-start(bf16[128,1024]{1,0:T(8,128)(2,1)} %param.17) | copy-start | bytes 786436
  7.2 119.7 %all-gather.9.cloned.1.call-start = ((), (), s32[]{:S(2)}) async-start(), calls=%async_computation.10 | async-start | bytes 1114112 | tf_op jit(solution)/shard_map/all_gather | solution.py:81
  7.9 121.5 %all-gather.7.cloned.1.call-start = ((), (), s32[]{:S(2)}) async-start(), calls=%async_computation.9 | async-start | bytes 3342336 | tf_op jit(solution)/shard_map/all_gather | solution.py:79
  8.7 142.4 %all-gather.11.cloned.1.call-start = ((), (), s32[]{:S(2)}) async-start(), calls=%async_computation.12 | async-start | bytes 4456448 | tf_op jit(solution)/shard_map/all_gather | solution.py:82
  9.4 190.8 %all-gather.13.cloned.1.call-start = ((), (), s32[]{:S(2)}) async-start(), calls=%async_computation.13 | async-start | bytes 4456448 | tf_op jit(solution)/shard_map/all_gather | solution.py:84
  10.0 248.0 %reduce-scatter.28.cloned.1.call-start = ((), (), s32[]{:S(2)}) async-start(), calls=%async_computation.21 | async-start | bytes 278528
  110.6 23.6 %copy-start.5 = (bf16[256,1024]{1,0:T(8,128)(2,1)}, bf16[256,1024]{1,0:T(8,128)(2,1)S(1)}, u32[]{:S(2)}) copy-start(bf16[256,1024]{1,0:T(8,128)(2,1)S(1)} %all_gather.51) | copy-start | bytes 1572868
  140.1 1.2 copy-start.1
  141.3 1.0 copy-start.3
  147.0 143.2 %reduce-scatter.16.cloned.1.call-start = ((), (), s32[]{:S(2)}) async-start(), calls=%async_computation.15 | async-start | bytes 786432 | tf_op jit(solution)/shard_map/reduce_scatter | solution.py:223
  150.9 139.8 %reduce-scatter.18.cloned.1.call-start = ((), (), s32[]{:S(2)}) async-start(), calls=%async_computation.16 | async-start | bytes 786432 | tf_op jit(solution)/shard_map/reduce_scatter | solution.py:226
  200.2 10.0 %copy-start.14 = (bf16[1024,2048]{1,0:T(8,128)(2,1)S(1)}, bf16[1024,2048]{1,0:T(8,128)(2,1)}, u32[]{:S(2)}) copy-start(bf16[1024,2048]{1,0:T(8,128)(2,1)} %all-gather.11.cloned.1.call-done) | copy-start | bytes 12582916
  209.2 1.0 copy-start.7
  212.3 95.1 %reduce-scatter.12.cloned.1.call-start = ((), (), s32[]{:S(2)}) async-start(), calls=%async_computation.11 | async-start | bytes 786432 | tf_op jit(solution)/shard_map/reduce_scatter | solution.py:133
  212.4 2.3 copy-start.2
  214.0 0.7 copy-start.11
  216.0 108.3 %reduce-scatter.14.cloned.1.call-start = ((), (), s32[]{:S(2)}) async-start(), calls=%async_computation.14 | async-start | bytes 786432 | tf_op jit(solution)/shard_map/reduce_scatter | solution.py:141
  216.0 3.5 copy-start.13
  219.6 2.2 copy-start.12
  221.7 1.9 copy-start.6
  221.7 169.0 %reduce-scatter.22.cloned.1.call-start = ((), (), s32[]{:S(2)}) async-start(), calls=%async_computation.18 | async-start | bytes 2228224 | tf_op jit(solution)/shard_map/reduce_scatter | solution.py:217
  223.6 256.4 %reduce-scatter.20.cloned.1.call-start = ((), (), s32[]{:S(2)}) async-start(), calls=%async_computation.17 | async-start | bytes 6684672 | tf_op jit(solution)/shard_map/reduce_scatter | solution.py:215
  227.4 360.8 %reduce-scatter.26.cloned.1.call-start = ((), (), s32[]{:S(2)}) async-start(), calls=%async_computation.20 | async-start | bytes 8912896 | tf_op jit(solution)/shard_map/reduce_scatter | solution.py:220
  231.9 1.0 copy-start.4
  231.9 1.4 copy-start.8
  232.0 465.2 %reduce-scatter.24.cloned.1.call-start = ((), (), s32[]{:S(2)}) async-start(), calls=%async_computation.19 | async-start | bytes 8912896 | tf_op jit(solution)/shard_map/reduce_scatter | solution.py:218
  237.8 0.7 copy-start.15
  237.8 52.8 %copy-start = (bf16[128,1024]{1,0:T(8,128)(2,1)S(1)}, bf16[128,1024]{1,0:T(8,128)(2,1)}, u32[]{:S(2)}) copy-start(bf16[128,1024]{1,0:T(8,128)(2,1)} %param.16) | copy-start | bytes 786436
  237.8 86.5 %copy-start.10 = (bf16[128,1024]{1,0:T(8,128)(2,1)S(1)}, bf16[128,1024]{1,0:T(8,128)(2,1)}, u32[]{:S(2)}) copy-start(bf16[128,1024]{1,0:T(8,128)(2,1)} %param.17) | copy-start | bytes 786436
  366.6 331.0 %copy-start.16 = (f32[32]{0:T(128)}, f32[32]{0:T(128)S(1)}, u32[]{:S(2)}) copy-start(f32[32]{0:T(128)S(1)} %dynamic-slice.4) | copy-start | bytes 388
Sparse Core Ops, SparseCore 0:
  10.2 40.7 all-gather.8
  53.1 44.3 all-gather.6
  99.7 49.3 all-gather.10
  151.1 49.0 all-gather.12
  204.1 53.7 reduce-scatter.27
  260.1 13.5 reduce-scatter.15
  276.0 14.5 reduce-scatter.17
  292.9 14.5 reduce-scatter.11
  309.8 14.5 reduce-scatter.13
  328.5 62.1 reduce-scatter.21
  395.7 84.1 reduce-scatter.19
  484.4 103.6 reduce-scatter.25
  592.8 104.3 reduce-scatter.23
where the time goes:
time: 705 us; the launch traced here: 704 us
  waiting for transfers between devices  425 us (60%)
  blocking collectives  176 us (25%)
  matrix products  48.5 us (7%)
  local copies, waits for them, and re-layouts  24.5 us (3%)
  between operations  15 us (2%)
  other arithmetic  14.6 us (2%)
    unnamed x3, blocking collectives  112 us
    reduce_scatter x1, waiting for transfers between devices, shards(): lax.psum_scatter(up_grad, 'dp', scatter_dimension=0, tiled=True)  109 us
    reduce_scatter x1, waiting for transfers between devices, shards(): lax.psum_scatter(down_grad, 'dp', scatter_dimension=0, tiled=True)  108 us
    reduce_scatter x1, waiting for transfers between devices, shards(): lax.psum_scatter(qkv_weight_grad, 'dp', scatter_dimension=0, tiled=True)  89.3 us
    all_gather x1, waiting for transfers between devices, shards(): lax.all_gather(down_weight, 'dp', axis=0, tiled=True)  44.1 us
    reduce_scatter x1, waiting for transfers between devices, shards(): lax.psum_scatter(dense_grad, 'dp', scatter_dimension=0, tiled=True)  21.7 us
    all_gather x1, blocking collectives, shards(): lax.all_gather(qkv_bias, 'dp', axis=1, tiled=True)  21.3 us
    unnamed x14, waiting for transfers between devices  21 us
  transfers between devices with their start and end apart: 13, of which 9 were waited for; matrix products, arithmetic and copies ran while one was open for 12% of the time, Pallas kernels for 0%

commit v1 on v0

--- a/solution.py
+++ b/solution.py
@@ -7,6 +7,18 @@
 ROT = 16
 NORM_EPS = 1e-05
 NEG_FILL = -1000000000.0
+
+
+def doubled_up(x, axis, dim):
+    ways, here = (lax.axis_size(axis), lax.axis_index(axis))
+    grown, reach = (x, 1)
+    while reach < ways:
+        theirs = lax.ppermute(grown, axis, [(d, d ^ reach) for d in range(ways)])
+        mine_first = jnp.concatenate([grown, theirs], axis=dim)
+        theirs_first = jnp.concatenate([theirs, grown], axis=dim)
+        grown = jnp.where(here & reach == 0, mine_first, theirs_first)
+        reach = 2 * reach
+    return grown
 
 
 def layer_norm(rows_in, gain_vec, shift_vec):
@@ -80,7 +92,7 @@
         lax.all_gather(qkv_bias, "dp", axis=1, tiled=True),
         lax.all_gather(dense_weight, "dp", axis=0, tiled=True),
         lax.all_gather(up_weight, "dp", axis=0, tiled=True),
-        lax.all_gather(up_bias, "dp", axis=0, tiled=True),
+        doubled_up(up_bias, "dp", 0),
         lax.all_gather(down_weight, "dp", axis=0, tiled=True),
     )
     model_width = full_qkv.shape[0]

time: 705 us -> 705 us (level)
  blocking collectives: 176 us -> 159 us
  waiting for transfers between devices: 425 us -> 442 us
    all_gather x1 -> x0, blocking collectives: 17.6 us -> none  [shards(): lax.all_gather(up_bias, 'dp', axis=0, tiled=True)]
    all_gather x1, waiting for transfers between devices: 0.02 us -> 11.3 us  [shards(): lax.all_gather(up_weight, 'dp', axis=0, tiled=True)]
    unnamed x56 -> x58, local copies, waits for them, and re-layouts: 16.8 us -> 16.7 us
  transfers between devices with their start and end apart: 13 -> 17, of which waited for: 9 -> 11; matrix products, arithmetic and copies ran while one was open for 12% -> 12% of each run, Pallas kernels for 0% -> 0%
where the time goes in v1:
time: 705 us; the launch traced here: 704 us
  waiting for transfers between devices  442 us (63%)
  blocking collectives  159 us (23%)
  matrix products  48.5 us (7%)
  local copies, waits for them, and re-layouts  24.4 us (3%)
  between operations  15 us (2%)
  other arithmetic  14.6 us (2%)
    unnamed x3, blocking collectives  112 us
    reduce_scatter x1, waiting for transfers between devices, shards(): lax.psum_scatter(up_grad, 'dp', scatter_dimension=0, tiled=True)  109 us
    reduce_scatter x1, waiting for transfers between devices, shards(): lax.psum_scatter(down_grad, 'dp', scatter_dimension=0, tiled=True)  108 us
    reduce_scatter x1, waiting for transfers between devices, shards(): lax.psum_scatter(qkv_weight_grad, 'dp', scatter_dimension=0, tiled=True)  89.3 us
    all_gather x1, waiting for transfers between devices, shards(): lax.all_gather(down_weight, 'dp', axis=0, tiled=True)  46.1 us
    reduce_scatter x1, waiting for transfers between devices, shards(): lax.psum_scatter(dense_grad, 'dp', scatter_dimension=0, tiled=True)  21.7 us
    all_gather x1, blocking collectives, shards(): lax.all_gather(qkv_bias, 'dp', axis=1, tiled=True)  21.4 us
    unnamed x14, waiting for transfers between devices  20.4 us
  transfers between devices with their start and end apart: 17, of which 11 were waited for; matrix products, arithmetic and copies ran while one was open for 12% of the time, Pallas kernels for 0%

profile of v1, /device:TPU:0, one launch (start us, length us, event | category | flops | bytes accessed | tf_op | source)
XLA Modules:
  0.0 704.5 jit_solution(11102197790374231231)
XLA Ops:
  7.2 0.7 all-gather.8.cloned.1.call-update
  8.0 0.7 all-gather.6.cloned.1.call-update
  8.7 0.7 all-gather.10.cloned.1.call-update
  10.1 0.7 bitcast_add_fusion
  10.7 0.8 dynamic-update-slice
  11.6 0.8 dynamic-update-slice.1
  12.4 0.8 dynamic-update-slice.2
  13.2 0.8 dynamic-update-slice.3
  14.1 0.8 dynamic-update-slice.4
  14.9 0.8 dynamic-update-slice.5
  15.7 42.2 %all-reduce.21 = (bf16[1024]{0:T(1024)(128)(2,1)S(1)}, bf16[1024]{0:T(1024)(128)(2,1)S(1)}, bf16[1024]{0:T(1024)(128)(2,1)S(1)}, bf16[1024]{0:T(1024)(128)(2,1)S...) all-reduce(bf16[1024]{0:T(1024)(128)(2,1)S(1)} %dynamic-update-slic, ...), channel_id=1, replica_groups=mesh['dp'=16,'tensor'=2] {'dp','tensor'}, use_global_device_ids=true, to_apply=%add.11 | all-reduce | flops 6144 | bytes 24576
  58.0 21.4 %all-gather = bf16[16,32,3]{1,2,0:T(4,128)(2,1)S(1)} all-gather(bf16[1,32,3]{1,2,0:T(4,128)(2,1)} %bitcast.93), channel_id=1, replica_groups=mesh['dp'=16,'tensor'=2] {'dp'}, dimensions={0}, use_global_device_ids=true | all-gather | bytes 3264 | tf_op jit(solution)/shard_map/all_gather | solution.py:92
  79.4 0.7 fusion.52
  80.1 1.1 convert_reduce_fusion.4
  81.2 1.2 fusion.28
  82.4 1.2 fusion.25
  83.6 9.2 %all_gather.48 = bf16[256,1024]{1,0:T(8,128)(2,1)S(1)} all-gather(bf16[128,1024]{1,0:T(8,128)(2,1)S(1)} %get-tuple-element.105), channel_id=1, replica_groups=mesh['dp'=16,'tensor'=2] {'tensor'}, dimensions={0}, use_global_device_ids=true | all-gather | bytes 786432 | tf_op jit(solution)/shard_map/all_gather | solution.py:87
  93.2 8.4 %all_gather.59 = bf16[256,1024]{1,0:T(8,128)(2,1)S(1)} all-gather(bf16[128,1024]{1,0:T(8,128)(2,1)S(1)} %copy-done.9), channel_id=1, replica_groups=mesh['dp'=16,'tensor'=2] {'tensor'}, dimensions={0}, use_global_device_ids=true | all-gather | bytes 786432 | tf_op jit(solution)/shard_map/all_gather | solution.py:157
  101.7 7.6 %all_gather.54 = bf16[256,1024]{1,0:T(8,128)(2,1)} all-gather(bf16[128,1024]{1,0:T(8,128)(2,1)S(1)} %get-tuple-element.106), channel_id=1, replica_groups=mesh['dp'=16,'tensor'=2] {'tensor'}, dimensions={0}, use_global_device_ids=true | all-gather | bytes 786432 | tf_op jit(solution)/shard_map/all_gather | solution.py:88
  109.5 4.3 collective-permute-done.3
  113.9 1.7 convolution_convert_fusion.4
  115.6 0.8 copy.71
  116.4 4.7 copy.67
  121.1 4.1 convolution_add_fusion
  125.2 1.9 copy.69
  127.4 0.9 copy-done.1
  129.3 1.6 multiply_reduce_fusion
  133.1 0.9 copy.84
  134.0 3.8 convolution_convert_fusion.2
  138.0 11.3 %all-gather.10.cloned.1.call-done = bf16[1024,2048]{1,0:T(8,128)(2,1)} async-done(((bf16[64,2048]{1,0:T(8,128)(2,1)}), bf16[1024,2048]{1,0:T(8,128)(2,1)}) %all-gather.10.cloned.1.call-update) | async-done | bytes 4194320 | tf_op jit(solution)/shard_map/all_gather | solution.py:94
  149.3 5.0 fusion.59
  154.3 46.1 %all-gather.12.cloned.1.call-done = bf16[2048,1024]{1,0:T(8,128)(2,1)} async-done(((bf16[128,1024]{1,0:T(8,128)(2,1)}), bf16[2048,1024]{1,0:T(8,128)(2,1)}) %all-gather.12.cloned.1.call-update) | async-done | bytes 4194320 | tf_op jit(solution)/shard_map/all_gather | solution.py:96
  200.4 9.1 %convert_reduce_fusion = (f32[2048]{0:T(1024)S(1)}, bf16[256,2048]{1,0:T(8,128)(2,1)S(1)}, f32[256,2048]{1,0:T(8,128)}) fusion(f32[256,2048]{1,0:T(8,128)} %fusion.59, f32[2048]{0:T(1024)S(1)} %fusion.51, bf16[256,1024]{1,0:T(8,128)(2,1)S(1)} %all_gather.59, bf16[2048,1024]{1,0:T(8,128)(2,1)} %all-gather.12.cloned.1.call-done), kind=kOutput, calls=%fused_computation.3 | convolution fusion | flops 1113061376 | bytes 9977856 | tf_op jit(solution)/shard_map/ld,fd->lf/dot_general | solution.py:166
  209.5 1.0 copy-done.7
  210.5 2.1 convolution_convert_fusion.1
  212.7 1.6 convolution_convert_fusion.5
  214.3 0.7 copy-done.11
  215.0 1.3 convolution_convert_fusion
  216.3 2.8 multiply_convert_fusion.1
  219.2 0.7 copy-done.14
  219.8 2.1 convolution_convert_fusion.3
  222.1 1.8 fusion.60
  223.9 3.7 fusion.36
  227.7 4.5 fusion.62
  232.3 1.0 copy-done.6
  233.6 4.5 fusion.61
  238.2 0.6 copy-done.16
  238.8 0.6 dynamic-slice.5
  240.0 18.2 %reduce-scatter.28.cloned.1.call-done = f32[32,3]{1,0:T(8,128)} async-done(((f32[512,3]{1,0:T(8,128)}), f32[32,3]{1,0:T(8,128)}) %reduce-scatter.28.cloned.1.call-update) | async-done | bytes 400
  258.2 1.4 copy.83
  259.5 30.2 %all-reduce.19 = f32[2048]{0:T(1024)S(1)} all-reduce(f32[2048]{0:T(1024)S(1)} %get-tuple-element.92), channel_id=15, replica_groups=mesh['dp'=16,'tensor'=2] {'dp'}, use_global_device_ids=true, to_apply=%region_30.31.clone | all-reduce | flops 2048 | bytes 16384
  289.7 0.6 dynamic-slice.6
  290.8 1.3 fusion.29
  292.2 1.6 fusion.35
  293.8 13.8 %reduce-scatter.12.cloned.1.call-done = bf16[128,1024]{1,0:T(8,128)(2,1)} async-done(((bf16[256,1024]{1,0:T(8,128)(2,1)}), bf16[128,1024]{1,0:T(8,128)(2,1)}) %reduce-scatter.12.cloned.1.call-update) | async-done | bytes 262160 | tf_op jit(solution)/shard_map/reduce_scatter | solution.py:145
  307.6 16.9 %reduce-scatter.14.cloned.1.call-done = bf16[128,1024]{1,0:T(8,128)(2,1)} async-done(((bf16[256,1024]{1,0:T(8,128)(2,1)}), bf16[128,1024]{1,0:T(8,128)(2,1)}) %reduce-scatter.14.cloned.1.call-update) | async-done | bytes 262160 | tf_op jit(solution)/shard_map/reduce_scatter | solution.py:153
  324.5 2.4 convert_reduce_fusion.5
  327.0 39.8 %all-reduce.20 = (f32[1024]{0:T(1024)S(1)}, f32[1024]{0:T(1024)S(1)}, f32[1024]{0:T(1024)S(1)}, f32[1024]{0:T(1024)S(1)}, f32[1024]{0:T(1024)S(1)}) all-reduce(f32[1024]{0:T(1024)S(1)} %get-tuple-element.76, f32[1024]{0:T(1024)S(1)} %get-tuple-element.80, ...), channel_id=6, replica_groups=mesh['dp'=16,'tensor'=2] {'dp','tensor'}, use_global_device_ids=true, to_apply=%region_15.16.clone | all-reduce | flops 5120 | bytes 40960
  366.8 0.6 dynamic-slice
  368.0 0.6 dynamic-slice.2
  369.1 21.7 %reduce-scatter.22.cloned.1.call-done = f32[32,1024]{1,0:T(8,128)} async-done(((f32[512,1024]{1,0:T(8,128)}), f32[32,1024]{1,0:T(8,128)}) %reduce-scatter.22.cloned.1.call-update) | async-done | bytes 131088 | tf_op jit(solution)/shard_map/reduce_scatter | solution.py:229
  390.9 89.3 %reduce-scatter.20.cloned.1.call-done = f32[64,3,512]{2,0,1:T(8,128)} async-done(((f32[1024,3,512]{2,0,1:T(8,128)}), f32[64,3,512]{2,0,1:T(8,128)}) %reduce-scatter.20.cloned.1.call-update) | async-done | bytes 393232 | tf_op jit(solution)/shard_map/reduce_scatter | solution.py:227
  480.1 108.3 %reduce-scatter.26.cloned.1.call-done = f32[128,1024]{1,0:T(8,128)} async-done(((f32[2048,1024]{1,0:T(8,128)}), f32[128,1024]{1,0:T(8,128)}) %reduce-scatter.26.cloned.1.call-update) | async-done | bytes 524304 | tf_op jit(solution)/shard_map/reduce_scatter | solution.py:232
  588.4 109.0 %reduce-scatter.24.cloned.1.call-done = f32[64,2048]{1,0:T(8,128)} async-done(((f32[1024,2048]{1,0:T(8,128)}), f32[64,2048]{1,0:T(8,128)}) %reduce-scatter.24.cloned.1.call-update) | async-done | bytes 524304 | tf_op jit(solution)/shard_map/reduce_scatter | solution.py:230
  (119 shorter events, 8.0 us)
Async XLA Ops:
  7.2 85.9 %copy-start.13 = (bf16[128]{0:T(256)(128)(2,1)S(1)}, bf16[128]{0:T(256)(128)(2,1)}, u32[]{:S(2)}) copy-start(bf16[128]{0:T(256)(128)(2,1)} %param.29) | copy-start | bytes 772
  7.2 86.0 %copy-start.9 = (bf16[128,1024]{1,0:T(8,128)(2,1)S(1)}, bf16[128,1024]{1,0:T(8,128)(2,1)}, u32[]{:S(2)}) copy-start(bf16[128,1024]{1,0:T(8,128)(2,1)} %param.17) | copy-start | bytes 786436
  7.2 106.7 %all-gather.8.cloned.1.call-start = ((), (), s32[]{:S(2)}) async-start(), calls=%async_computation.10 | async-start | bytes 1114112 | tf_op jit(solution)/shard_map/all_gather | solution.py:93
  7.9 108.5 %all-gather.6.cloned.1.call-start = ((), (), s32[]{:S(2)}) async-start(), calls=%async_computation.9 | async-start | bytes 3342336 | tf_op jit(solution)/shard_map/all_gather | solution.py:91
  8.7 140.6 %all-gather.10.cloned.1.call-start = ((), (), s32[]{:S(2)}) async-start(), calls=%async_computation.12 | async-start | bytes 4456448 | tf_op jit(solution)/shard_map/all_gather | solution.py:94
  9.4 191.0 %all-gather.12.cloned.1.call-start = ((), (), s32[]{:S(2)}) async-start(), calls=%async_computation.13 | async-start | bytes 4456448 | tf_op jit(solution)/shard_map/all_gather | solution.py:96
  9.5 83.6 %collective-permute-start = (bf16[128]{0:T(256)(128)(2,1)}, bf16[128]{0:T(256)(128)(2,1)S(1)}, u32[]{:S(2)}, u32[]{:S(2)}) collective-permute-start(bf16[128]{0:T(256)(128)(2,1)} %param.29), channel_id=1, source_target_pairs={{0,2},{2,0},{4,6},{6,4},{8,10},{10,8},{12,14},{14,12},{16,18},{18,... | collective-permute-start | bytes 776 | tf_op jit(solution)/shard_map/ppermute | solution.py:16
  10.0 248.2 %reduce-scatter.28.cloned.1.call-start = ((), (), s32[]{:S(2)}) async-start(), calls=%async_computation.21 | async-start | bytes 278528
  92.8 28.3 %copy-start.4 = (bf16[256,1024]{1,0:T(8,128)(2,1)}, bf16[256,1024]{1,0:T(8,128)(2,1)S(1)}, u32[]{:S(2)}) copy-start(bf16[256,1024]{1,0:T(8,128)(2,1)S(1)} %all_gather.48) | copy-start | bytes 1572868
  93.1 8.5 %collective-permute-start.1 = (bf16[256]{0:T(256)(128)(2,1)S(1)}, bf16[256]{0:T(256)(128)(2,1)S(1)}, u32[]{:S(2)}, u32[]{:S(2)}) collective-permute-start(bf16[256]{0:T(256)(128)(2,1)S(1)} %broadcast_select_fusion), channel_id=1, source_target_pairs={{0,4},{2,6},{4,0},{6,2},{8,12},{10,14},{12,8},{14,10},{16,20},{18,... | collective-permute-start | bytes 1544 | tf_op jit(solution)/shard_map/ppermute | solution.py:16
  101.6 7.7 %collective-permute-start.2 = (bf16[512]{0:T(512)(128)(2,1)S(1)}, bf16[512]{0:T(512)(128)(2,1)S(1)}, u32[]{:S(2)}, u32[]{:S(2)}) collective-permute-start(bf16[512]{0:T(512)(128)(2,1)S(1)} %maximum_select_fusion.2), channel_id=1, source_target_pairs={{0,8},{2,10},{4,12},{6,14},{8,0},{10,2},{12,4},{14,6},{16,24},{18,... | collective-permute-start | bytes 3080 | tf_op jit(solution)/shard_map/ppermute | solution.py:16
  109.3 4.6 collective-permute-start.3
  127.1 1.2 copy-start.1
  128.3 0.9 copy-start.3
  134.0 156.4 %reduce-scatter.16.cloned.1.call-start = ((), (), s32[]{:S(2)}) async-start(), calls=%async_computation.15 | async-start | bytes 786432 | tf_op jit(solution)/shard_map/reduce_scatter | solution.py:235
  137.8 153.0 %reduce-scatter.18.cloned.1.call-start = ((), (), s32[]{:S(2)}) async-start(), calls=%async_computation.16 | async-start | bytes 786432 | tf_op jit(solution)/shard_map/reduce_scatter | solution.py:238
  200.4 10.1 %copy-start.15 = (bf16[1024,2048]{1,0:T(8,128)(2,1)S(1)}, bf16[1024,2048]{1,0:T(8,128)(2,1)}, u32[]{:S(2)}) copy-start(bf16[1024,2048]{1,0:T(8,128)(2,1)} %all-gather.10.cloned.1.call-done) | copy-start | bytes 12582916
  209.5 1.0 copy-start.7
  212.6 95.0 %reduce-scatter.12.cloned.1.call-start = ((), (), s32[]{:S(2)}) async-start(), calls=%async_computation.11 | async-start | bytes 786432 | tf_op jit(solution)/shard_map/reduce_scatter | solution.py:145
  212.7 2.3 copy-start.2
  214.3 0.7 copy-start.11
  216.3 108.3 %reduce-scatter.14.cloned.1.call-start = ((), (), s32[]{:S(2)}) async-start(), calls=%async_computation.14 | async-start | bytes 786432 | tf_op jit(solution)/shard_map/reduce_scatter | solution.py:153
  216.3 3.5 copy-start.14
  219.8 2.2 copy-start.12
  222.0 1.9 copy-start.5
  222.0 168.9 %reduce-scatter.22.cloned.1.call-start = ((), (), s32[]{:S(2)}) async-start(), calls=%async_computation.18 | async-start | bytes 2228224 | tf_op jit(solution)/shard_map/reduce_scatter | solution.py:229
  223.9 256.3 %reduce-scatter.20.cloned.1.call-start = ((), (), s32[]{:S(2)}) async-start(), calls=%async_computation.17 | async-start | bytes 6684672 | tf_op jit(solution)/shard_map/reduce_scatter | solution.py:227
  227.6 360.8 %reduce-scatter.26.cloned.1.call-start = ((), (), s32[]{:S(2)}) async-start(), calls=%async_computation.20 | async-start | bytes 8912896 | tf_op jit(solution)/shard_map/reduce_scatter | solution.py:232
  232.2 1.0 copy-start.6
  232.2 1.4 copy-start.8
  232.2 465.2 %reduce-scatter.24.cloned.1.call-start = ((), (), s32[]{:S(2)}) async-start(), calls=%async_computation.19 | async-start | bytes 8912896 | tf_op jit(solution)/shard_map/reduce_scatter | solution.py:230
  238.1 0.7 copy-start.16
  238.1 52.7 %copy-start = (bf16[128,1024]{1,0:T(8,128)(2,1)S(1)}, bf16[128,1024]{1,0:T(8,128)(2,1)}, u32[]{:S(2)}) copy-start(bf16[128,1024]{1,0:T(8,128)(2,1)} %param.16) | copy-start | bytes 786436
  238.1 86.4 %copy-start.10 = (bf16[128,1024]{1,0:T(8,128)(2,1)S(1)}, bf16[128,1024]{1,0:T(8,128)(2,1)}, u32[]{:S(2)}) copy-start(bf16[128,1024]{1,0:T(8,128)(2,1)} %param.17) | copy-start | bytes 786436
  366.8 331.1 %copy-start.17 = (f32[32]{0:T(128)}, f32[32]{0:T(128)S(1)}, u32[]{:S(2)}) copy-start(f32[32]{0:T(128)S(1)} %dynamic-slice.4) | copy-start | bytes 388
Sparse Core Ops, SparseCore 0:
  10.2 40.7 all-gather.7
  53.2 44.3 all-gather.5
  99.7 49.5 all-gather.9
  151.3 49.0 all-gather.11
  204.4 53.7 reduce-scatter.27
  260.3 13.5 reduce-scatter.15
  276.2 14.5 reduce-scatter.17
  293.1 14.5 reduce-scatter.11
  310.0 14.5 reduce-scatter.13
  328.7 62.1 reduce-scatter.21
  395.9 84.1 reduce-scatter.19
  484.6 103.7 reduce-scatter.25
  593.0 104.3 reduce-scatter.23
